TPU v7x, 512 devices: a whole 4x4x16 slice. The times are simulated.
512 devices in a mesh: dp: 8 (over y, core), ctx: 64 (over z, x).
Axes of the slice: x: 4, y: 4, z: 16, core: 2. Of those that a mesh axis runs over, the one named last changes fastest.
Arguments:
- queries: bfloat16 [8, 8192, 1024], P('dp', 'ctx'), may hold values from -6 to 6
- keys: bfloat16 [8, 8192, 1024], P('dp', 'ctx'), may hold values from -6 to 6
- values: bfloat16 [8, 8192, 1024], P('dp', 'ctx'), may hold values from -6 to 6
- log_decay: float32 [8, 8, 8192], P('dp', None, 'ctx'), may hold values from -2 to 0
- gain: float32 [1024], replicated, may hold values from 0.1 to 1.9
- out_grad: bfloat16 [8, 8192, 1024], P('dp', 'ctx'), may hold values from -16 to 16
Outputs:
- query_grad: bfloat16 [8, 8192, 1024], P('dp', 'ctx')
- key_grad: bfloat16 [8, 8192, 1024], P('dp', 'ctx')
- value_grad: bfloat16 [8, 8192, 1024], P('dp', 'ctx')
- gain_grad: float32 [1024], P('ctx')
All inputs are finite; a program needn't handle non-finite values.
Results may differ from a plain program's by a relative error of at most 0.0059.
Values sent between devices are 32-bit elements; how exact they have to be, the bound alone decides.
A program may use at most 128 MiB of HBM per device.

v0:
```python
import jax
import jax.numpy as jnp
from jax import lax
from jax.sharding import PartitionSpec as P

EPSILON = 1e-06


def prefix(part, axis, combine, identity, reverse):
    count = lax.axis_size(axis)
    place = lax.axis_index(axis)
    ahead = count - 1 - place if reverse else place
    gathered = jax.tree.map(lambda a: lax.all_gather(a, axis), part)
    state = jax.tree.map(lambda a, e: jnp.zeros_like(a) + jnp.asarray(e, a.dtype), part, identity)

    def one(step, state):
        source = count - 1 - step if reverse else step
        return combine(
            state, jax.tree.map(lambda a: lax.dynamic_index_in_dim(a, source, 0, False), gathered)
        )

    return lax.fori_loop(0, ahead, one, state)


def combine(earlier, latter):
    earlier_decay, earlier_state = earlier
    latter_decay, latter_state = latter
    return (
        earlier_decay * latter_decay,
        latter_decay[..., None, None] * earlier_state + latter_state,
    )


def causal_decay(cumulative):
    length = cumulative.shape[-1]
    causal = jnp.tril(jnp.ones((length, length), dtype=bool))
    spread = cumulative[..., :, None] - cumulative[..., None, :]
    return jnp.where(causal, jnp.exp(jnp.where(causal, spread, 0.0)), 0.0)


def body(queries, keys, values, log_decay, gain, out_grad):
    batch_rows, length, full_width = queries.shape
    head_count = log_decay.shape[1]
    head_size = full_width // head_count
    query_heads = queries.reshape(batch_rows, length, head_count, head_size)
    key_heads = keys.reshape(batch_rows, length, head_count, head_size)
    value_heads = values.reshape(batch_rows, length, head_count, head_size)
    cumulative = jnp.cumsum(log_decay, axis=2)
    from_start = jnp.exp(cumulative).transpose(0, 2, 1)[..., None]
    to_end = jnp.exp(cumulative[..., -1:] - cumulative).transpose(0, 2, 1)[..., None]
    key_decayed = (key_heads * to_end).astype(jnp.bfloat16)
    block_state = jnp.einsum(
        "bthi,bthj->bhij", key_decayed, value_heads, preferred_element_type=jnp.float32
    )
    block_decay = jnp.exp(cumulative[..., -1])
    start_decay = jnp.ones_like(block_decay)
    start_state = jnp.zeros_like(block_state)
    entering = prefix(
        (block_decay, block_state), "ctx", combine, (start_decay, start_state), False
    )[1]
    entering_half = entering.astype(jnp.bfloat16)
    decay_mask = causal_decay(cumulative)
    scores = jnp.einsum(
        "bthi,bshi->bhts", query_heads, key_heads, preferred_element_type=jnp.float32
    )
    weights = (scores * decay_mask).astype(jnp.bfloat16)
    attended = from_start * jnp.einsum(
        "bthi,bhij->bthj", query_heads, entering_half, preferred_element_type=jnp.float32
    )
    attended = attended + jnp.einsum(
        "bhts,bshj->bthj", weights, value_heads, preferred_element_type=jnp.float32
    )
    root_mean = jnp.sqrt(jnp.mean(attended * attended, axis=-1, keepdims=True) + EPSILON)
    normed = attended / root_mean
    upstream = out_grad.reshape(batch_rows, length, head_count, head_size).astype(jnp.float32)
    scaled_up = gain.reshape(head_count, head_size) * upstream
    attended_grad = (
        (scaled_up - normed * jnp.mean(scaled_up * normed, axis=-1, keepdims=True)) / root_mean
    ).astype(jnp.bfloat16)
    gain_terms = jnp.sum(upstream * normed, axis=(0, 1)).reshape(full_width)
    portion = full_width // lax.axis_size("ctx")
    summed = lax.psum(gain_terms, ("dp", "ctx"))
    gain_grad = lax.dynamic_slice_in_dim(summed, lax.axis_index("ctx") * portion, portion)
    grad_scores = jnp.einsum(
        "bthj,bshj->bhts", attended_grad, value_heads, preferred_element_type=jnp.float32
    )
    grad_weights = (grad_scores * decay_mask).astype(jnp.bfloat16)
    query_grad = from_start * jnp.einsum(
        "bthj,bhij->bthi", attended_grad, entering_half, preferred_element_type=jnp.float32
    )
    query_grad = query_grad + jnp.einsum(
        "bhts,bshi->bthi", grad_weights, key_heads, preferred_element_type=jnp.float32
    )
    query_decayed = (query_heads * from_start).astype(jnp.bfloat16)
    block_adjoint = jnp.einsum(
        "bthi,bthj->bhij", query_decayed, attended_grad, preferred_element_type=jnp.float32
    )
    returned = prefix(
        (block_decay, block_adjoint), "ctx", combine, (start_decay, start_state), True
    )[1]
    returned_half = returned.astype(jnp.bfloat16)
    key_grad = to_end * jnp.einsum(
        "bthj,bhij->bthi", value_heads, returned_half, preferred_element_type=jnp.float32
    )
    key_grad = key_grad + jnp.einsum(
        "bhts,bthi->bshi", grad_weights, query_heads, preferred_element_type=jnp.float32
    )
    value_grad = to_end * jnp.einsum(
        "bthi,bhij->bthj", key_heads, returned_half, preferred_element_type=jnp.float32
    )
    value_grad = value_grad + jnp.einsum(
        "bhts,bthj->bshj", weights, attended_grad, preferred_element_type=jnp.float32
    )
    return (
        query_grad.reshape(batch_rows, length, full_width).astype(jnp.bfloat16),
        key_grad.reshape(batch_rows, length, full_width).astype(jnp.bfloat16),
        value_grad.reshape(batch_rows, length, full_width).astype(jnp.bfloat16),
        gain_grad,
    )


def solution(mesh):
    in_specs = (
        P("dp", "ctx", None),
        P("dp", "ctx", None),
        P("dp", "ctx", None),
        P("dp", None, "ctx"),
        P(),
        P("dp", "ctx", None),
    )
    out_specs = (P("dp", "ctx", None), P("dp", "ctx", None), P("dp", "ctx", None), P("ctx"))
    return jax.shard_map(body, mesh=mesh, in_specs=in_specs, out_specs=out_specs, check_vma=False)
```

profile of v0, /device:TPU:1, one launch (start us, length us, event | category | flops | bytes accessed | tf_op | source)
XLA Modules:
  0.0 764.6 jit_solution(14405945986678790667)
XLA Ops:
  11.9 71.4 %all-gather = f32[64,8,1]{1,2,0:T(1,128)S(1)} all-gather(f32[1,8,1]{1,2,0:T(1,128)S(1)} %copy.61), channel_id=2, replica_groups=mesh['dp'=8,'ctx'=64] {'ctx'}, dimensions={0}, use_global_device_ids=true | all-gather | bytes 2080 | tf_op jit(solution)/shard_map/all_gather | solution.py:13
  86.4 224.8 %all-gather.6.cloned.1.call-done = f32[512,128,128]{2,1,0:T(8,128)} async-done(((f32[8,128,128]{2,1,0:T(8,128)}), f32[512,128,128]{2,1,0:T(8,128)}) %all-gather.6.cloned.1.call-update) | async-done | bytes 33554448 | tf_op jit(solution)/shard_map/all_gather | solution.py:13
  316.4 177.8 %psum.7 = f32[1024]{0:T(1024)S(1)} all-reduce(f32[1024]{0:T(1024)S(1)} %bitcast.158), channel_id=1, replica_groups=mesh['dp'=8,'ctx'=64] {'dp','ctx'}, use_global_device_ids=true, to_apply=%region_8.9 | all-reduce | flops 1024 | bytes 8192 | tf_op jit(solution)/shard_map/psum | solution.py:82
  495.2 182.3 %all-gather.8.cloned.1.call-done = f32[512,128,128]{2,1,0:T(8,128)} async-done(((f32[8,128,128]{2,1,0:T(8,128)}), f32[512,128,128]{2,1,0:T(8,128)}) %all-gather.8.cloned.1.call-update) | async-done | bytes 33554448 | tf_op jit(solution)/shard_map/all_gather | solution.py:13
  677.6 77.8 %while.27 = (s32[]{:T(128)}, f32[1,8,128,128]{3,2,1,0:T(8,128)S(1)}, s32[]{:T(128)}, f32[64,1,8]{2,1,0:T(1,128)S(1)}, f32[64,1,8,128,128]{4,3,2,1,0:T(8,128)}, /*index=5*/s32[]{:T(128)}, s32[]{:T(128)}, s32[]{:T(128)}, s32[]{:T(128)}) while((s32[]{:T(128)}, f32[1,8,128,128]{3,2,1,0:T(8,128)S(1)}, s32[]{:T(128)}, f32[64,1,8]{2,1,0:T(1,128)S(1)}, ...), condition=%wide.region_6.7_spmd, body=%wide.region_5.6_spmd.sunk | while | flops 262150 | bytes 1573107 | solution.py:22
  677.6 1.2 bitcast_add_fusion.5
  678.8 1.2 bitcast_add_fusion.5
  680.1 1.2 bitcast_add_fusion.5
  681.3 1.2 bitcast_add_fusion.5
  682.5 1.2 bitcast_add_fusion.5
  683.8 1.2 bitcast_add_fusion.5
  685.0 1.2 bitcast_add_fusion.5
  686.2 1.2 bitcast_add_fusion.5
  687.5 1.2 bitcast_add_fusion.5
  688.7 1.2 bitcast_add_fusion.5
  689.9 1.2 bitcast_add_fusion.5
  691.2 1.2 bitcast_add_fusion.5
  692.4 1.2 bitcast_add_fusion.5
  693.6 1.2 bitcast_add_fusion.5
  694.9 1.2 bitcast_add_fusion.5
  696.1 1.2 bitcast_add_fusion.5
  697.4 1.2 bitcast_add_fusion.5
  698.6 1.2 bitcast_add_fusion.5
  699.8 1.2 bitcast_add_fusion.5
  701.1 1.2 bitcast_add_fusion.5
  702.3 1.2 bitcast_add_fusion.5
  703.5 1.2 bitcast_add_fusion.5
  704.8 1.2 bitcast_add_fusion.5
  706.0 1.2 bitcast_add_fusion.5
  707.2 1.2 bitcast_add_fusion.5
  708.5 1.2 bitcast_add_fusion.5
  709.7 1.2 bitcast_add_fusion.5
  710.9 1.2 bitcast_add_fusion.5
  712.2 1.2 bitcast_add_fusion.5
  713.4 1.2 bitcast_add_fusion.5
  714.6 1.2 bitcast_add_fusion.5
  715.9 1.2 bitcast_add_fusion.5
  717.1 1.2 bitcast_add_fusion.5
  718.3 1.2 bitcast_add_fusion.5
  719.6 1.2 bitcast_add_fusion.5
  720.8 1.2 bitcast_add_fusion.5
  722.0 1.2 bitcast_add_fusion.5
  723.3 1.2 bitcast_add_fusion.5
  724.5 1.2 bitcast_add_fusion.5
  725.8 1.2 bitcast_add_fusion.5
  727.0 1.2 bitcast_add_fusion.5
  728.2 1.2 bitcast_add_fusion.5
  729.5 1.2 bitcast_add_fusion.5
  730.7 1.2 bitcast_add_fusion.5
  731.9 1.2 bitcast_add_fusion.5
  733.2 1.2 bitcast_add_fusion.5
  734.4 1.2 bitcast_add_fusion.5
  735.6 1.2 bitcast_add_fusion.5
  736.9 1.2 bitcast_add_fusion.5
  738.1 1.2 bitcast_add_fusion.5
  739.3 1.2 bitcast_add_fusion.5
  740.6 1.2 bitcast_add_fusion.5
  741.8 1.2 bitcast_add_fusion.5
  743.0 1.2 bitcast_add_fusion.5
  744.3 1.2 bitcast_add_fusion.5
  748.0 1.2 bitcast_add_fusion.5
  749.2 1.2 bitcast_add_fusion.5
  750.4 1.2 bitcast_add_fusion.5
  751.7 1.2 bitcast_add_fusion.5
  (106 shorter events, 21.4 us)
Async XLA Ops:
  7.2 304.0 %all-gather.6.cloned.1.call-start = ((), (), s32[]{:S(2)}) async-start(), calls=%async_computation | async-start | bytes 34078720 | tf_op jit(solution)/shard_map/all_gather | solution.py:13
  11.7 665.8 %all-gather.8.cloned.1.call-start = ((), (), s32[]{:S(2)}) async-start(), calls=%async_computation.1 | async-start | bytes 34078720 | tf_op jit(solution)/shard_map/all_gather | solution.py:13
Sparse Core Ops, SparseCore 0:
  11.8 299.2 all-gather.5
  314.8 362.6 all-gather.7
where the time goes:
time: 768 us; the launch traced here: 765 us
  waiting for transfers between devices  407 us (53%)
  blocking collectives  249 us (32%)
  other arithmetic  78 us (10%)
  between operations  14.2 us (2%)
  local copies, waits for them, and re-layouts  8.53 us (1%)
    all_gather x2, waiting for transfers between devices, prefix(): gathered = jax.tree.map(lambda a: lax.all_gather(a, axis), part)  407 us
    psum x1, blocking collectives, body(): summed = lax.psum(gain_terms, ('dp', 'ctx'))  178 us
    add x63, other arithmetic, combine(): latter_decay[..., None, None] * earlier_state + latter_state  75 us
    all_gather x1, blocking collectives, prefix(): gathered = jax.tree.map(lambda a: lax.all_gather(a, axis), part)  71.4 us
  transfers between devices with their start and end apart: 2, of which 2 were waited for; matrix products, arithmetic and copies ran while one was open for 1% of the time, Pallas kernels for 0%

commit v1 on v0

--- a/solution.py
+++ b/solution.py
@@ -79,7 +79,10 @@
     ).astype(jnp.bfloat16)
     gain_terms = jnp.sum(upstream * normed, axis=(0, 1)).reshape(full_width)
     portion = full_width // lax.axis_size("ctx")
-    summed = lax.psum(gain_terms, ("dp", "ctx"))
+    recast_sources_all = lambda tile_in, axis_name: jnp.sum(
+        jax.lax.all_gather(tile_in, axis_name), axis=0
+    )
+    summed = recast_sources_all(gain_terms, ("dp", "ctx"))
     gain_grad = lax.dynamic_slice_in_dim(summed, lax.axis_index("ctx") * portion, portion)
     grad_scores = jnp.einsum(
         "bthj,bshj->bhts", attended_grad, value_heads, preferred_element_type=jnp.float32

time: 768 us -> 958 us (1.25)
  waiting for transfers between devices: 407 us -> 772 us
  blocking collectives: 249 us -> 71.4 us
    all_gather x0 -> x1, waiting for transfers between devices: none -> 258 us  [body(): jax.lax.all_gather(tile_in, axis_name)]
    psum x1 -> x0, blocking collectives: 178 us -> none  [body(): summed = lax.psum(gain_terms, ('dp', 'ctx'))]
    all_gather x2, waiting for transfers between devices: 407 us -> 514 us  [prefix(): gathered = jax.tree.map(lambda a: lax.all_gather(a, axis), part)]
  transfers between devices with their start and end apart: 2 -> 3, of which waited for: 2 -> 3; matrix products, arithmetic and copies ran while one was open for 1% -> 1% of each run, Pallas kernels for 0% -> 0%
where the time goes in v1:
time: 958 us; the launch traced here: 954 us
  waiting for transfers between devices  772 us (81%)
  other arithmetic  81.4 us (8%)
  blocking collectives  71.4 us (7%)
  between operations  13.9 us (1%)
    all_gather x2, waiting for transfers between devices, prefix(): gathered = jax.tree.map(lambda a: lax.all_gather(a, axis), part)  514 us
    all_gather x1, waiting for transfers between devices, body(): jax.lax.all_gather(tile_in, axis_name)  258 us
    add x63, other arithmetic, combine(): latter_decay[..., None, None] * earlier_state + latter_state  75 us
    all_gather x1, blocking collectives, prefix(): gathered = jax.tree.map(lambda a: lax.all_gather(a, axis), part)  71.4 us
  transfers between devices with their start and end apart: 3, of which 3 were waited for; matrix products, arithmetic and copies ran while one was open for 1% of the time, Pallas kernels for 0%

profile of v1, /device:TPU:1, one launch (start us, length us, event | category | flops | bytes accessed | tf_op | source)
XLA Modules:
  0.0 954.3 jit_solution(3904094104519826624)
XLA Ops:
  11.9 71.4 %all-gather = f32[64,8,1]{1,2,0:T(1,128)S(1)} all-gather(f32[1,8,1]{1,2,0:T(1,128)S(1)} %copy.61), channel_id=2, replica_groups=mesh['dp'=8,'ctx'=64] {'ctx'}, dimensions={0}, use_global_device_ids=true | all-gather | bytes 2080 | tf_op jit(solution)/shard_map/all_gather | solution.py:13
  86.4 224.8 %all-gather.8.cloned.1.call-done = f32[512,128,128]{2,1,0:T(8,128)} async-done(((f32[8,128,128]{2,1,0:T(8,128)}), f32[512,128,128]{2,1,0:T(8,128)}) %all-gather.8.cloned.1.call-update) | async-done | bytes 33554448 | tf_op jit(solution)/shard_map/all_gather | solution.py:13
  311.6 1.6 multiply_reduce_fusion
  317.5 257.8 %all-gather.12.cloned.1.call-done = f32[512,1,1024]{2,1,0:T(1,128)} async-done(((f32[1,1,1024]{2,1,0:T(1,128)}), f32[512,1,1024]{2,1,0:T(1,128)}) %all-gather.12.cloned.1.call-update) | async-done | bytes 2097168 | tf_op jit(solution)/shard_map/all_gather | solution.py:83
  575.3 2.8 reduce_sum.39
  578.7 288.9 %all-gather.10.cloned.1.call-done = f32[512,128,128]{2,1,0:T(8,128)} async-done(((f32[8,128,128]{2,1,0:T(8,128)}), f32[512,128,128]{2,1,0:T(8,128)}) %all-gather.10.cloned.1.call-update) | async-done | bytes 33554448 | tf_op jit(solution)/shard_map/all_gather | solution.py:13
  867.6 77.8 %while.27 = (s32[]{:T(128)}, f32[1,8,128,128]{3,2,1,0:T(8,128)S(1)}, s32[]{:T(128)}, f32[64,1,8]{2,1,0:T(1,128)S(1)}, f32[64,1,8,128,128]{4,3,2,1,0:T(8,128)}, /*index=5*/s32[]{:T(128)}, s32[]{:T(128)}, s32[]{:T(128)}, s32[]{:T(128)}) while((s32[]{:T(128)}, f32[1,8,128,128]{3,2,1,0:T(8,128)S(1)}, s32[]{:T(128)}, f32[64,1,8]{2,1,0:T(1,128)S(1)}, ...), condition=%wide.region_6.7_spmd, body=%wide.region_5.6_spmd.sunk | while | flops 262150 | bytes 1573107 | solution.py:22
  867.6 1.2 bitcast_add_fusion.5
  868.9 1.2 bitcast_add_fusion.5
  870.1 1.2 bitcast_add_fusion.5
  871.3 1.2 bitcast_add_fusion.5
  872.6 1.2 bitcast_add_fusion.5
  873.8 1.2 bitcast_add_fusion.5
  875.0 1.2 bitcast_add_fusion.5
  876.3 1.2 bitcast_add_fusion.5
  877.5 1.2 bitcast_add_fusion.5
  878.8 1.2 bitcast_add_fusion.5
  880.0 1.2 bitcast_add_fusion.5
  881.2 1.2 bitcast_add_fusion.5
  882.5 1.2 bitcast_add_fusion.5
  883.7 1.2 bitcast_add_fusion.5
  884.9 1.2 bitcast_add_fusion.5
  886.2 1.2 bitcast_add_fusion.5
  887.4 1.2 bitcast_add_fusion.5
  888.6 1.2 bitcast_add_fusion.5
  889.9 1.2 bitcast_add_fusion.5
  891.1 1.2 bitcast_add_fusion.5
  892.3 1.2 bitcast_add_fusion.5
  893.6 1.2 bitcast_add_fusion.5
  894.8 1.2 bitcast_add_fusion.5
  896.0 1.2 bitcast_add_fusion.5
  897.3 1.2 bitcast_add_fusion.5
  898.5 1.2 bitcast_add_fusion.5
  899.7 1.2 bitcast_add_fusion.5
  901.0 1.2 bitcast_add_fusion.5
  902.2 1.2 bitcast_add_fusion.5
  903.4 1.2 bitcast_add_fusion.5
  904.7 1.2 bitcast_add_fusion.5
  905.9 1.2 bitcast_add_fusion.5
  907.2 1.2 bitcast_add_fusion.5
  908.4 1.2 bitcast_add_fusion.5
  909.6 1.2 bitcast_add_fusion.5
  910.9 1.2 bitcast_add_fusion.5
  912.1 1.2 bitcast_add_fusion.5
  913.3 1.2 bitcast_add_fusion.5
  914.6 1.2 bitcast_add_fusion.5
  915.8 1.2 bitcast_add_fusion.5
  917.0 1.2 bitcast_add_fusion.5
  918.3 1.2 bitcast_add_fusion.5
  919.5 1.2 bitcast_add_fusion.5
  920.7 1.2 bitcast_add_fusion.5
  922.0 1.2 bitcast_add_fusion.5
  924.4 1.2 bitcast_add_fusion.5
  925.7 1.2 bitcast_add_fusion.5
  926.9 1.2 bitcast_add_fusion.5
  928.1 1.2 bitcast_add_fusion.5
  931.8 1.2 bitcast_add_fusion.5
  933.1 1.2 bitcast_add_fusion.5
  934.3 1.2 bitcast_add_fusion.5
  935.6 1.2 bitcast_add_fusion.5
  939.3 1.2 bitcast_add_fusion.5
  940.5 1.2 bitcast_add_fusion.5
  941.7 1.2 bitcast_add_fusion.5
  943.0 1.2 bitcast_add_fusion.5
  (109 shorter events, 22.8 us)
Async XLA Ops:
  7.2 304.0 %all-gather.8.cloned.1.call-start = ((), (), s32[]{:S(2)}) async-start(), calls=%async_computation | async-start | bytes 34078720 | tf_op jit(solution)/shard_map/all_gather | solution.py:13
  11.7 563.6 %all-gather.12.cloned.1.call-start = ((), (), s32[]{:S(2)}) async-start(), calls=%async_computation.2 | async-start | bytes 2101248 | tf_op jit(solution)/shard_map/all_gather | solution.py:83
  313.2 554.3 %all-gather.10.cloned.1.call-start = ((), (), s32[]{:S(2)}) async-start(), calls=%async_computation.1 | async-start | bytes 34078720 | tf_op jit(solution)/shard_map/all_gather | solution.py:13
Sparse Core Ops, SparseCore 0:
  11.8 299.2 all-gather.7
  316.4 258.9 all-gather.11
  578.3 289.2 all-gather.9
